TPU v7x, 32 devices: a whole 2x2x4 slice. The times are simulated.
32 devices in a mesh: dp: 8 (over z, x), mp: 4 (over y, core).
Axes of the slice: x: 2, y: 2, z: 4, core: 2. Of those that a mesh axis runs over, the one named last changes fastest.
Arguments:
- block_in: bfloat16 [16384, 1024], P('dp', 'mp')
- out_grad: bfloat16 [16384, 1024], P('dp', 'mp')
- lengths: int32 [16], P('dp'), may hold values from 256 to 1024
- group_ids: int32 [16], P('dp'), may hold values from 0 to 7
- time_embed: float32 [8, 1024], replicated, may hold values from -6 to 6
- weights: float32 [1024, 14, 1024], P('dp', None, 'mp')
- first_moments: float32 [1024, 14, 1024], P('dp', None, 'mp')
- second_moments: float32 [1024, 14, 1024], P('dp', None, 'mp'), as said below
- owners: int32 [14, 8], replicated, may hold values from 0 to 7, each once within a row
- left_basis: float32 [14, 1024, 128], P(None, 'dp'), may hold values from -1 to 1, as said below
- right_basis: float32 [14, 1024, 256], P(None, 'mp'), may hold values from -1 to 1, as said below
- biases: float32 [13, 1024], P(None, 'mp'), may hold values from -2.5 to 2.5
- bias_first: float32 [13, 1024], P(None, 'mp')
- bias_second: float32 [13, 1024], P(None, 'mp'), as said below
Outputs:
- block_out: bfloat16 [16384, 1024], P('dp', 'mp')
- input_grad: float32 [16384, 1024], P('dp', 'mp')
- weight_grads: float32 [1024, 14, 1024], P('dp', None, 'mp')
- new_first: float32 [1024, 14, 1024], P('dp', None, 'mp')
- new_second: float32 [1024, 14, 1024], P('dp', None, 'mp')
- new_weights: float32 [1024, 14, 1024], P('dp', None, 'mp')
- new_weights_low: bfloat16 [1024, 14, 1024], P('dp', None, 'mp')
- new_bias_first: float32 [13, 1024], P(None, 'mp')
- new_bias_second: float32 [13, 1024], P(None, 'mp')
- new_biases: float32 [13, 1024], P(None, 'mp')
Inputs may be any that keep to these rules, and one draw needn't show every extreme that they name: Each block left_basis[k, a * 128 to a * 128 + 127, :] is an orthogonal matrix. Each block right_basis[k, c * 256 to c * 256 + 255, :] is an orthogonal matrix. `second_moments`: positive. `bias_second`: positive.
All inputs are finite; a program needn't handle non-finite values.
Results may differ from a plain program's by a relative error of at most 0.02.
The roundings to bfloat16 on the way count: a program that leaves them out, or rounds other values in their place, can miss the bound.
Values may be sent and summed in bfloat16 or wider, within the bound.
No kernel may reach another device: no remote copies, remote signals or barrier semaphores. Data moves between devices by JAX's collectives and lax.ppermute only.
A program may use at most 192 MiB of HBM per device.

v0:
```python
import jax
import jax.numpy as jnp
from jax import lax
from jax.sharding import PartitionSpec as P

D = 1024
HEAD_DIM = 64
LEN = 1024
UTT_DEV = 2
GROUPS = 8
STEP = 10
norm_epsilon = 1e-06
soap_first = 0.95
soap_second = 0.95
soap_epsilon = 1e-08
soap_rate = 0.05
soap_decay = 0.01
vector_first = 0.9
vector_second = 0.999
vector_epsilon = 1e-08
vector_rate = 0.1
masked_score = -1e30


def true_order(gathered, owners):
    block_count = owners.shape[1]
    blocks = gathered.reshape(
        block_count, gathered.shape[0] // block_count, gathered.shape[1], gathered.shape[2]
    )
    picked = [
        jnp.take(blocks[:, :, slot_index, :], owners[slot_index], axis=0)
        for slot_index in range(owners.shape[0])
    ]
    return jnp.stack(picked, axis=2).reshape(gathered.shape)


def stored_order(values, owners):
    block_count = owners.shape[1]
    blocks = values.reshape(
        block_count, values.shape[0] // block_count, values.shape[1], values.shape[2]
    )
    placed = [
        jnp.take(blocks[:, :, slot_index, :], jnp.argsort(owners[slot_index]), axis=0)
        for slot_index in range(owners.shape[0])
    ]
    return jnp.stack(placed, axis=2).reshape(values.shape)


def gather_block(low_weights, owners):
    whole_rows = lax.all_gather(low_weights[:, :8, :], "dp", axis=0, tiled=True)
    return true_order(whole_rows, owners[:8])


def reduce_grads(values):
    return lax.psum_scatter(
        values.astype(jnp.bfloat16), "dp", scatter_dimension=0, tiled=True
    ).astype(jnp.float32)


def branch_total(partial_rows):
    return lax.psum_scatter(
        partial_rows.astype(jnp.bfloat16), "mp", scatter_dimension=1, tiled=True
    ).astype(jnp.float32)


def branch_spread(grad_rows):
    return lax.all_gather(grad_rows, "mp", axis=1, tiled=True)


def gelu_tanh(values):
    return jax.nn.gelu(values, approximate=True)


def rotary_tables():
    half_dim = HEAD_DIM // 2
    places = jnp.arange(LEN, dtype=jnp.float32)
    frequencies = 10000.0 ** (-(jnp.arange(half_dim, dtype=jnp.float32) * 2.0 / HEAD_DIM))
    angles = places[:, None] * frequencies[None, :]
    return (jnp.cos(angles)[:, None, :], jnp.sin(angles)[:, None, :])


def rotate(values, cosine_table, sine_table, direction_sign):
    pair_view = values.reshape(values.shape[0], values.shape[1], values.shape[2] // 2, 2)
    even_part = pair_view[..., 0]
    odd_part = pair_view[..., 1]
    turned = jnp.stack(
        [
            even_part * cosine_table - direction_sign * odd_part * sine_table,
            odd_part * cosine_table + direction_sign * even_part * sine_table,
        ],
        axis=-1,
    )
    return turned.reshape(values.shape)


def modulated(values, shift_row, scale_row):
    totals = lax.psum((jnp.sum(values, axis=1), jnp.sum(values * values, axis=1)), "mp")
    row_mean = totals[0] / D
    spread = totals[1] / D - row_mean * row_mean
    inverse = lax.rsqrt(spread + norm_epsilon)
    normed = (values - row_mean[:, None]) * inverse[:, None]
    low_rows = (normed * (1.0 + scale_row) + shift_row).astype(jnp.bfloat16)
    return (lax.all_gather(low_rows, "mp", axis=1, tiled=True), normed, inverse)


def norm_back(partial_rows, normed, inverse, scale_row):
    grad_hidden = lax.psum_scatter(
        partial_rows.astype(jnp.bfloat16), "mp", scatter_dimension=1, tiled=True
    ).astype(jnp.float32)
    grad_normed = grad_hidden * (1.0 + scale_row)
    totals = lax.psum((jnp.sum(grad_normed, axis=1), jnp.sum(grad_normed * normed, axis=1)), "mp")
    grad_rows = inverse[:, None] * (
        grad_normed - totals[0][:, None] / D - normed * totals[1][:, None] / D
    )
    return (grad_rows, jnp.sum(grad_hidden, axis=0), jnp.sum(grad_hidden * normed, axis=0))


def attend(queries, keys_in, values_in, valid_rows):
    score_scale = HEAD_DIM ** (-0.5)
    block_rows = LEN // 2
    outputs = []
    totals = []
    for offset in range(0, LEN, block_rows):
        scores = (
            jnp.einsum(
                "qhd,khd->hqk",
                queries[offset : offset + block_rows],
                keys_in,
                preferred_element_type=jnp.float32,
            )
            * score_scale
        )
        scores = jnp.where(valid_rows[None, None, :], scores, masked_score)
        row_top = jnp.max(scores, axis=2, keepdims=True)
        row_total = row_top + jnp.log(jnp.sum(jnp.exp(scores - row_top), axis=2, keepdims=True))
        chances = jnp.exp(scores - row_total).astype(jnp.bfloat16)
        outputs.append(
            jnp.einsum("hqk,khd->qhd", chances, values_in, preferred_element_type=jnp.float32)
        )
        totals.append(row_total)
    return (jnp.concatenate(outputs, axis=0).astype(jnp.bfloat16), totals)


def attend_back(queries, keys_in, values_in, valid_rows, totals, grad_mixed):
    score_scale = HEAD_DIM ** (-0.5)
    block_rows = LEN // 2
    grad_keys = jnp.zeros(keys_in.shape, jnp.float32)
    grad_values = jnp.zeros(values_in.shape, jnp.float32)
    grad_queries = []
    for position, offset in enumerate(range(0, LEN, block_rows)):
        query_rows = queries[offset : offset + block_rows]
        grad_rows = grad_mixed[offset : offset + block_rows]
        scores = (
            jnp.einsum("qhd,khd->hqk", query_rows, keys_in, preferred_element_type=jnp.float32)
            * score_scale
        )
        scores = jnp.where(valid_rows[None, None, :], scores, masked_score)
        soft_chances = jnp.exp(scores - totals[position])
        grad_values = grad_values + jnp.einsum(
            "hqk,qhd->khd",
            soft_chances.astype(jnp.bfloat16),
            grad_rows,
            preferred_element_type=jnp.float32,
        )
        grad_chances = jnp.einsum(
            "qhd,khd->hqk", grad_rows, values_in, preferred_element_type=jnp.float32
        )
        inner = jnp.sum(soft_chances * grad_chances, axis=2, keepdims=True)
        grad_scores = (soft_chances * (grad_chances - inner)).astype(jnp.bfloat16)
        grad_queries.append(
            jnp.einsum("hqk,khd->qhd", grad_scores, keys_in, preferred_element_type=jnp.float32)
            * score_scale
        )
        grad_keys = (
            grad_keys
            + jnp.einsum(
                "hqk,qhd->khd", grad_scores, query_rows, preferred_element_type=jnp.float32
            )
            * score_scale
        )
    return (jnp.concatenate(grad_queries, axis=0), grad_keys, grad_values)


def body(
    block_in,
    out_grad,
    lengths,
    group_ids,
    time_embed,
    weights,
    first_moments,
    second_moments,
    owners,
    left_basis,
    right_basis,
    biases,
    bias_first,
    bias_second,
):
    highest = lax.Precision.HIGHEST
    shard_width = weights.shape[2]
    head_count = shard_width // HEAD_DIM
    group_hits = (group_ids[:, None] == jnp.arange(GROUPS, dtype=jnp.int32)[None, :]).astype(
        jnp.float32
    )
    embedded = jnp.dot(group_hits, time_embed, precision=highest)
    condition = jax.nn.silu(embedded).astype(jnp.bfloat16)
    low_weights = weights.astype(jnp.bfloat16)
    mod_whole = lax.all_gather(low_weights[:, 8:, :], "dp", axis=0, tiled=True)
    mod_true = true_order(mod_whole, owners[8:])
    modulation = (
        jnp.einsum("ud,dkc->ukc", condition, mod_true, preferred_element_type=jnp.float32)
        + biases[7:]
    )
    cosine_table, sine_table = rotary_tables()
    outputs = []
    input_rows = []
    mod_grads = []
    weight_total = jnp.zeros((D, 8, shard_width), jnp.float32)
    bias_total = jnp.zeros((7, shard_width), jnp.float32)
    for utterance in range(UTT_DEV):
        block_now = gather_block(low_weights, owners)
        mod_row = modulation[utterance]
        rows_x = block_in[utterance * LEN : (utterance + 1) * LEN].astype(jnp.float32)
        cotangent = out_grad[utterance * LEN : (utterance + 1) * LEN].astype(jnp.float32)
        valid_rows = jnp.arange(LEN, dtype=jnp.int32) < lengths[utterance]
        keep_rows = valid_rows.astype(jnp.float32)[:, None]
        normed_in, first_norm, first_inverse = modulated(rows_x, mod_row[0], mod_row[1])
        projected = (
            jnp.einsum(
                "td,dkc->tkc", normed_in, block_now[:, 0:3, :], preferred_element_type=jnp.float32
            )
            + biases[0:3]
        )
        queries = rotate(
            projected[:, 0, :].reshape(LEN, head_count, HEAD_DIM), cosine_table, sine_table, 1.0
        ).astype(jnp.bfloat16)
        keys_in = rotate(
            projected[:, 1, :].reshape(LEN, head_count, HEAD_DIM), cosine_table, sine_table, 1.0
        ).astype(jnp.bfloat16)
        values_in = projected[:, 2, :].reshape(LEN, head_count, HEAD_DIM).astype(jnp.bfloat16)
        mixed, totals = attend(queries, keys_in, values_in, valid_rows)
        mixed_rows = mixed.reshape(LEN, shard_width)
        attended = (
            branch_total(
                jnp.einsum(
                    "tc,oc->to", mixed_rows, block_now[:, 3, :], preferred_element_type=jnp.float32
                )
            )
            + biases[3]
        ) * keep_rows
        middle = rows_x + mod_row[2] * attended
        normed_mid, second_norm, second_inverse = modulated(middle, mod_row[3], mod_row[4])
        hidden = (
            jnp.einsum(
                "td,dec->tec", normed_mid, block_now[:, 4:6, :], preferred_element_type=jnp.float32
            )
            + biases[4:6]
        )
        active = gelu_tanh(hidden).astype(jnp.bfloat16)
        fed_rows = (
            branch_total(
                jnp.einsum(
                    "tec,oec->to", active, block_now[:, 6:8, :], preferred_element_type=jnp.float32
                )
            )
            + biases[6]
        )
        outputs.append((middle + mod_row[5] * fed_rows).astype(jnp.bfloat16))
        grad_fed = (mod_row[5] * cotangent).astype(jnp.bfloat16)
        grad_fed_whole = branch_spread(grad_fed)
        grad_out_weight = jnp.einsum(
            "to,tec->oec", grad_fed_whole, active, preferred_element_type=jnp.float32
        )
        grad_active = jnp.einsum(
            "to,oec->tec", grad_fed_whole, block_now[:, 6:8, :], preferred_element_type=jnp.float32
        )
        grad_hidden = jax.vjp(gelu_tanh, hidden)[1](grad_active)[0].astype(jnp.bfloat16)
        grad_in_weight = jnp.einsum(
            "td,tec->dec", normed_mid, grad_hidden, preferred_element_type=jnp.float32
        )
        grad_mid_norm, shift_two, scale_two = norm_back(
            jnp.einsum(
                "tec,dec->td", grad_hidden, block_now[:, 4:6, :], preferred_element_type=jnp.float32
            ),
            second_norm,
            second_inverse,
            mod_row[4],
        )
        grad_middle = cotangent + grad_mid_norm
        grad_attended = (mod_row[2] * grad_middle * keep_rows).astype(jnp.bfloat16)
        grad_attended_whole = branch_spread(grad_attended)
        grad_proj_weight = jnp.einsum(
            "to,tc->oc", grad_attended_whole, mixed_rows, preferred_element_type=jnp.float32
        )
        grad_mixed = jnp.einsum(
            "to,oc->tc", grad_attended_whole, block_now[:, 3, :], preferred_element_type=jnp.float32
        ).astype(jnp.bfloat16)
        grad_query_turned, grad_key_turned, grad_values = attend_back(
            queries,
            keys_in,
            values_in,
            valid_rows,
            totals,
            grad_mixed.reshape(LEN, head_count, HEAD_DIM),
        )
        grad_projected = jnp.stack(
            [
                rotate(grad_query_turned, cosine_table, sine_table, -1.0).reshape(LEN, shard_width),
                rotate(grad_key_turned, cosine_table, sine_table, -1.0).reshape(LEN, shard_width),
                grad_values.reshape(LEN, shard_width),
            ],
            axis=1,
        ).astype(jnp.bfloat16)
        grad_qkv_weight = jnp.einsum(
            "td,tkc->dkc", normed_in, grad_projected, preferred_element_type=jnp.float32
        )
        grad_in_norm, shift_one, scale_one = norm_back(
            jnp.einsum(
                "tkc,dkc->td",
                grad_projected,
                block_now[:, 0:3, :],
                preferred_element_type=jnp.float32,
            ),
            first_norm,
            first_inverse,
            mod_row[1],
        )
        input_rows.append(grad_middle + grad_in_norm)
        mod_grads.append(
            jnp.stack(
                [
                    shift_one,
                    scale_one,
                    jnp.sum(grad_middle * attended, axis=0),
                    shift_two,
                    scale_two,
                    jnp.sum(cotangent * fed_rows, axis=0),
                ]
            )
        )
        weight_total = weight_total + jnp.concatenate(
            [grad_qkv_weight, grad_proj_weight[:, None, :], grad_in_weight, grad_out_weight], axis=1
        )
        bias_total = bias_total + jnp.concatenate(
            [
                jnp.sum(grad_projected.astype(jnp.float32), axis=0),
                jnp.sum(grad_attended.astype(jnp.float32), axis=0)[None, :],
                jnp.sum(grad_hidden.astype(jnp.float32), axis=0),
                jnp.sum(grad_fed.astype(jnp.float32), axis=0)[None, :],
            ],
            axis=0,
        )
    grad_mods = jnp.stack(mod_grads)
    grad_mod_weight = jnp.einsum(
        "ud,ukc->dkc", condition.astype(jnp.float32), grad_mods, precision=highest
    )
    reduced = reduce_grads(
        stored_order(jnp.concatenate([weight_total, grad_mod_weight], axis=1), owners)
    )
    bias_local = jnp.concatenate([bias_total, jnp.sum(grad_mods, axis=0)], axis=0)
    bias_grad = lax.psum(bias_local, "dp")
    turned = jnp.einsum("kij,ikc->jkc", left_basis, reduced, precision=highest)
    turned = jnp.einsum("jkc,kce->jke", turned, right_basis, precision=highest)
    first_new = soap_first * first_moments + (1.0 - soap_first) * turned
    second_new = soap_second * second_moments + (1.0 - soap_second) * turned * turned
    direction = (
        first_new
        / (1.0 - soap_first**STEP)
        / (jnp.sqrt(second_new / (1.0 - soap_second**STEP)) + soap_epsilon)
    )
    rotated_back = jnp.einsum("kij,jke->ike", left_basis, direction, precision=highest)
    rotated_back = jnp.einsum("ike,kce->ikc", rotated_back, right_basis, precision=highest)
    new_weights = weights - soap_rate * (rotated_back + soap_decay * weights)
    bias_first_new = vector_first * bias_first + (1.0 - vector_first) * bias_grad
    bias_second_new = vector_second * bias_second + (1.0 - vector_second) * bias_grad * bias_grad
    new_biases = biases - vector_rate * (bias_first_new / (1.0 - vector_first**STEP)) / (
        jnp.sqrt(bias_second_new / (1.0 - vector_second**STEP)) + vector_epsilon
    )
    return (
        jnp.concatenate(outputs, axis=0),
        jnp.concatenate(input_rows, axis=0),
        reduced,
        first_new,
        second_new,
        new_weights,
        new_weights.astype(jnp.bfloat16),
        bias_first_new,
        bias_second_new,
        new_biases,
    )


def solution(mesh):
    return jax.shard_map(
        body,
        mesh=mesh,
        in_specs=(
            P("dp", "mp"),
            P("dp", "mp"),
            P("dp"),
            P("dp"),
            P(),
            P("dp", None, "mp"),
            P("dp", None, "mp"),
            P("dp", None, "mp"),
            P(),
            P(None, "dp", None),
            P(None, "mp", None),
            P(None, "mp"),
            P(None, "mp"),
            P(None, "mp"),
        ),
        out_specs=(
            P("dp", "mp"),
            P("dp", "mp"),
            P("dp", None, "mp"),
            P("dp", None, "mp"),
            P("dp", None, "mp"),
            P("dp", None, "mp"),
            P("dp", None, "mp"),
            P(None, "mp"),
            P(None, "mp"),
            P(None, "mp"),
        ),
        check_vma=False,
    )
```

profile of v0, /device:TPU:0, one launch (start us, length us, event | category | flops | bytes accessed | tf_op | source)
XLA Modules:
  0.0 1064.8 jit_solution(13720281788594007767)
XLA Ops:
  13.4 12.6 %all-reduce.3 = (f32[1024]{0:T(1024)S(1)}, f32[1024]{0:T(1024)S(1)}, f32[1024]{0:T(1024)S(1)}, f32[1024]{0:T(1024)S(1)}) all-reduce(f32[1024]{0:T(1024)S(1)} %get-tuple-element.61, f32[1024]{0:T(1024)S(1)} %get-tuple-element.60, f32[1024]{0:T(1024)S(1)} %get-tuple-element.62, ...), channel_id=1, replica_groups=mesh['dp'=8,'mp'=4] {'mp'}, use_global_device_ids=true, to_apply=%region_3.5 | all-reduce | flops 4096 | bytes 32768 | tf_op jit(solution)/shard_map/psum | solution.py:97
  26.9 47.2 %all-gather.11.cloned.1.call-done = bf16[1024,6,256]{2,0,1:T(8,128)(2,1)} async-done(((bf16[128,6,256]{2,0,1:T(8,128)(2,1)}), bf16[1024,6,256]{2,0,1:T(8,128)(2,1)}) %all-gather.11.cloned.1.call-update) | async-done | bytes 3145744 | tf_op jit(solution)/shard_map/all_gather | solution.py:209
  74.1 3.2 slice_bitcast_fusion.22
  99.7 48.6 %all-gather.15.cloned.1.call-done = bf16[1024,8,256]{2,0,1:T(8,128)(2,1)} async-done(((bf16[128,8,256]{2,0,1:T(8,128)(2,1)}), bf16[1024,8,256]{2,0,1:T(8,128)(2,1)}) %all-gather.15.cloned.1.call-update) | async-done | bytes 4194320 | tf_op jit(solution)/shard_map/all_gather | solution.py:50
  148.3 3.8 slice_bitcast_fusion.17
  171.6 3.8 fusion.59
  177.0 19.5 %all-gather.19.cloned.1.call-done = bf16[1024,1024]{1,0:T(8,128)(2,1)} async-done(((bf16[1024,256]{1,0:T(8,128)(2,1)}), bf16[1024,1024]{1,0:T(8,128)(2,1)}) %all-gather.19.cloned.1.call-update) | async-done | bytes 2097168 | tf_op jit(solution)/shard_map/all_gather | solution.py:103
  196.5 3.7 fusion.62
  213.7 8.6 subtract_convert_fusion.4
  225.5 3.4 fusion.131
  233.2 3.4 exponential_reduce_fusion.1
  247.3 2.9 pad_maximum_fusion.10
  251.5 3.5 fusion.132
  259.4 3.4 exponential_reduce_fusion.3
  274.8 4.0 reduce-scatter.14.cloned.1.call-done
  278.8 34.6 %reduce-scatter.10.cloned.1.call-done = bf16[1024,256]{1,0:T(8,128)(2,1)} async-done(((bf16[1024,1024]{1,0:T(8,128)(2,1)}), bf16[1024,256]{1,0:T(8,128)(2,1)}) %reduce-scatter.10.cloned.1.call-update) | async-done | bytes 524304 | tf_op jit(solution)/shard_map/reduce_scatter | solution.py:61
  315.6 10.1 all-reduce.2
  325.8 3.0 add_convert_fusion.3
  328.9 3.1 convert_reduce_fusion.10
  346.2 6.7 all-gather.21.cloned.1.call-done
  352.8 4.5 fusion.32
  357.3 20.5 %all-gather.27.cloned.1.call-done = bf16[1024,1024]{1,0:T(8,128)(2,1)} async-done(((bf16[1024,256]{1,0:T(8,128)(2,1)}), bf16[1024,1024]{1,0:T(8,128)(2,1)}) %all-gather.27.cloned.1.call-update) | async-done | bytes 2097168 | tf_op jit(solution)/shard_map/all_gather | solution.py:67
  377.8 5.4 convert_reduce_fusion.2
  386.9 16.0 %all-gather.17.cloned.1.call-done = bf16[1024,1024]{1,0:T(8,128)(2,1)} async-done(((bf16[1024,256]{1,0:T(8,128)(2,1)}), bf16[1024,1024]{1,0:T(8,128)(2,1)}) %all-gather.17.cloned.1.call-update) | async-done | bytes 2097168 | tf_op jit(solution)/shard_map/all_gather | solution.py:103
  402.8 4.4 fusion.40
  407.2 19.9 %all-gather.23.cloned.1.call-done = bf16[1024,1024]{1,0:T(8,128)(2,1)} async-done(((bf16[1024,256]{1,0:T(8,128)(2,1)}), bf16[1024,1024]{1,0:T(8,128)(2,1)}) %all-gather.23.cloned.1.call-update) | async-done | bytes 2097168 | tf_op jit(solution)/shard_map/all_gather | solution.py:67
  427.1 5.4 convert_reduce_fusion.3
  436.4 4.7 bitcast_convert_fusion.4
  441.2 4.8 bitcast_convert_fusion.5
  461.1 34.0 %reduce-scatter.18.cloned.1.call-done = bf16[1024,256]{1,0:T(8,128)(2,1)} async-done(((bf16[1024,1024]{1,0:T(8,128)(2,1)}), bf16[1024,256]{1,0:T(8,128)(2,1)}) %reduce-scatter.18.cloned.1.call-update) | async-done | bytes 524304 | tf_op jit(solution)/shard_map/reduce_scatter | solution.py:107
  498.0 10.1 all-reduce.1
  508.1 21.0 %reduce-scatter.16.cloned.1.call-done = bf16[1024,256]{1,0:T(8,128)(2,1)} async-done(((bf16[1024,1024]{1,0:T(8,128)(2,1)}), bf16[1024,256]{1,0:T(8,128)(2,1)}) %reduce-scatter.16.cloned.1.call-update) | async-done | bytes 524304 | tf_op jit(solution)/shard_map/reduce_scatter | solution.py:61
  529.2 34.0 %reduce-scatter.12.cloned.1.call-done = bf16[1024,256]{1,0:T(8,128)(2,1)} async-done(((bf16[1024,1024]{1,0:T(8,128)(2,1)}), bf16[1024,256]{1,0:T(8,128)(2,1)}) %reduce-scatter.12.cloned.1.call-update) | async-done | bytes 524304 | tf_op jit(solution)/shard_map/reduce_scatter | solution.py:61
  563.1 4.2 convert_reduce_fusion.11
  569.8 3.9 convert_reduce_fusion.13
  573.8 16.6 %all-gather.29.cloned.1.call-done = bf16[1024,1024]{1,0:T(8,128)(2,1)} async-done(((bf16[1024,256]{1,0:T(8,128)(2,1)}), bf16[1024,1024]{1,0:T(8,128)(2,1)}) %all-gather.29.cloned.1.call-update) | async-done | bytes 2097168 | tf_op jit(solution)/shard_map/all_gather | solution.py:67
  593.6 4.5 fusion.199
  598.1 14.9 %multiply_reduce_fusion = (f32[4,512]{1,0:T(4,128)S(1)}, f32[4,512]{1,0:T(4,128)S(1)}, f32[4,512,1024]{2,1,0:T(8,128)}) fusion(f32[4,512,1024]{2,1,0:T(8,128)} %copy-done.3, f32[4,512]{1,0:T(4,128)S(1)} %log_add_fusion, pred[1024]{0:T(1024)(128)(4,1)S(1)} %iota_compare_fusion, f32[4,512,1024]{2,1,0:T(8,128)} %fusion.199, f32[4,512]{1,0:T(4,128)S(1)} %log_add_fusion.1, ...), kind=kOutput, calls=%fused_computation.31 | convolution fusion | flops 289402880 | bytes 34374656 | tf_op jit(solution)/shard_map/qhd,khd->hqk/dot_general | solution.py:165
  615.2 9.9 multiply_convert_fusion
  635.2 4.5 fusion.197
  639.8 14.1 %multiply_reduce_fusion.2 = (f32[4,512]{1,0:T(4,128)S(1)}, f32[4,512]{1,0:T(4,128)S(1)}, f32[4,512,1024]{2,1,0:T(8,128)}) fusion(f32[4,512,1024]{2,1,0:T(8,128)} %copy-done.2, f32[4,512]{1,0:T(4,128)S(1)} %log_add_fusion.2, pred[1024]{0:T(1024)(128)(4,1)S(1)} %iota_compare_fusion.1, f32[4,512,1024]{2,1,0:T(8,128)} %fusion.197, ...), kind=kOutput, calls=%fused_computation.35 | convolution fusion | flops 289402880 | bytes 34374656 | tf_op jit(solution)/shard_map/qhd,khd->hqk/dot_general | solution.py:165
  656.1 10.3 multiply_convert_fusion.2
  670.5 6.1 fusion.88
  678.7 4.5 fusion.92
  693.1 4.5 fusion.90
  707.3 8.5 subtract_convert_fusion.3
  721.8 3.1 pad_maximum_fusion.17
  729.0 4.9 bitcast_convert_fusion
  734.2 5.4 fusion.142
  739.6 6.6 fusion.87
  748.2 3.1 pad_maximum_fusion.14
  755.4 2.9 pad_maximum_fusion.15
  761.6 5.0 bitcast_convert_fusion.2
  767.0 4.6 fusion.30
  788.7 8.9 maximum_add_fusion
  802.2 10.1 all-reduce
  812.4 3.2 multiply_reduce_fusion.5
  815.7 4.2 fusion.146
  820.0 6.7 pad_maximum_fusion
  826.7 5.7 slice_bitcast_fusion
  911.5 39.7 %psum.135 = f32[13,256]{1,0:T(8,128)S(1)} all-reduce(f32[13,256]{1,0:T(8,128)S(1)} %pad_maximum_fusion.24), channel_id=1, replica_groups=mesh['dp'=8,'mp'=4] {'dp'}, use_global_device_ids=true, to_apply=%region_87.90 | all-reduce | flops 3328 | bytes 26624 | tf_op jit(solution)/shard_map/psum | solution.py:362
  956.6 85.2 %reduce-scatter.26.cloned.1.call-done = bf16[128,14,256]{2,0,1:T(8,128)(2,1)} async-done(((bf16[1024,14,256]{2,0,1:T(8,128)(2,1)}), bf16[128,14,256]{2,0,1:T(8,128)(2,1)}) %reduce-scatter.26.cloned.1.call-update) | async-done | bytes 917520 | tf_op jit(solution)/shard_map/reduce_scatter | solution.py:55
  1044.1 4.3 fusion.46
  1051.3 5.4 fusion.196
  (644 shorter events, 318.9 us)
Async XLA Ops:
  7.2 1034.7 %copy-start = (f32[14,128,128]{2,1,0:T(8,128)S(1)}, f32[14,128,128]{2,1,0:T(8,128)}, u32[]{:S(2)}) copy-start(f32[14,128,128]{2,1,0:T(8,128)} %param.27) | copy-start | bytes 2752516
  7.2 18.8 %copy-start.78 = (s32[14,8]{0,1:T(8,128)S(1)}, s32[14,8]{0,1:T(8,128)}, u32[]{:S(2)}) copy-start(s32[14,8]{0,1:T(8,128)} %param.26) | copy-start | bytes 1348
  7.2 19.4 %copy-start.130 = (f32[8,1024]{1,0:T(8,128)S(1)}, f32[8,1024]{1,0:T(8,128)}, u32[]{:S(2)}) copy-start(f32[8,1024]{1,0:T(8,128)} %param.22) | copy-start | bytes 98308
  7.2 19.4 %copy-start.131 = (s32[2]{0:T(128)S(1)}, s32[2]{0:T(128)}, u32[]{:S(2)}) copy-start(s32[2]{0:T(128)} %param.21) | copy-start | bytes 28
  7.2 66.9 %all-gather.11.cloned.1.call-start = ((), (), s32[]{:S(2)}) async-start(), calls=%async_computation.9 | async-start | bytes 3538944 | tf_op jit(solution)/shard_map/all_gather | solution.py:209
  10.7 137.6 %all-gather.15.cloned.1.call-start = ((), (), s32[]{:S(2)}) async-start(), calls=%async_computation.11 | async-start | bytes 4718592 | tf_op jit(solution)/shard_map/all_gather | solution.py:50
  12.7 158.9 %all-gather.13.cloned.1.call-start = ((), (), s32[]{:S(2)}) async-start(), calls=%async_computation.10 | async-start | bytes 2621440 | tf_op jit(solution)/shard_map/all_gather | solution.py:103
  26.7 67.5 %copy-start.95 = (f32[1024]{0:T(1024)}, f32[1024]{0:T(1024)S(1)}, u32[]{:S(2)}) copy-start(f32[1024]{0:T(1024)S(1)} %get-tuple-element.293) | copy-start | bytes 12292
  26.7 67.5 %copy-start.97 = (f32[1024]{0:T(1024)}, f32[1024]{0:T(1024)S(1)}, u32[]{:S(2)}) copy-start(f32[1024]{0:T(1024)S(1)} %get-tuple-element.294) | copy-start | bytes 12292
  26.7 67.5 %copy-start.101 = (f32[1024]{0:T(1024)}, f32[1024]{0:T(1024)S(1)}, u32[]{:S(2)}) copy-start(f32[1024]{0:T(1024)S(1)} %get-tuple-element.224) | copy-start | bytes 12292
  26.7 67.5 %copy-start.103 = (f32[1024]{0:T(1024)}, f32[1024]{0:T(1024)S(1)}, u32[]{:S(2)}) copy-start(f32[1024]{0:T(1024)S(1)} %get-tuple-element.225) | copy-start | bytes 12292
  26.9 66.6 %copy-start.109 = (bf16[2,1024]{1,0:T(2,128)(2,1)}, bf16[2,1024]{1,0:T(2,128)(2,1)S(1)}, u32[]{:S(2)}) copy-start(bf16[2,1024]{1,0:T(2,128)(2,1)S(1)} %fusion.150) | copy-start | bytes 12292
  94.1 58.1 %copy-start.105 = (f32[1,1,256]{2,0,1:T(1,128)}, f32[1,1,256]{2,0,1:T(1,128)S(1)}, u32[]{:S(2)}) copy-start(f32[1,1,256]{2,0,1:T(1,128)S(1)} %get-tuple-element.218) | copy-start | bytes 3076
  94.1 58.1 %copy-start.107 = (f32[1,1,256]{2,0,1:T(1,128)}, f32[1,1,256]{2,0,1:T(1,128)S(1)}, u32[]{:S(2)}) copy-start(f32[1,1,256]{2,0,1:T(1,128)S(1)} %get-tuple-element.213) | copy-start | bytes 3076
  95.8 100.6 %all-gather.19.cloned.1.call-start = ((), (), s32[]{:S(2)}) async-start(), calls=%async_computation.15 | async-start | bytes 2621440 | tf_op jit(solution)/shard_map/all_gather | solution.py:103
  97.8 180.9 %reduce-scatter.14.cloned.1.call-start = ((), (), s32[]{:S(2)}) async-start(), calls=%async_computation.16 | async-start | bytes 2621440 | tf_op jit(solution)/shard_map/reduce_scatter | solution.py:61
  99.7 114.0 %copy-start.71 = (f32[1024,32]{0,1:T(8,128)}, f32[1024,32]{0,1:T(8,128)S(1)}, u32[]{:S(2)}) copy-start(f32[1024,32]{0,1:T(8,128)S(1)} %get-tuple-element.234) | copy-start | bytes 393220
  175.4 21.0 %copy-start.80 = (bf16[1024,1,256]{0,2,1:T(8,128)(2,1)S(1)}, bf16[1024,1,256]{0,2,1:T(8,128)(2,1)}, u32[]{:S(2)}) copy-start(bf16[1024,1,256]{0,2,1:T(8,128)(2,1)} %copy.67) | copy-start | bytes 1572868
  175.5 92.6 %copy-start.21 = (bf16[1024,1,256]{0,2,1:T(8,128)(2,1)}, bf16[1024,1,256]{0,2,1:T(8,128)(2,1)S(1)}, u32[]{:S(2)}) copy-start(bf16[1024,1,256]{0,2,1:T(8,128)(2,1)S(1)} %slice.800) | copy-start | bytes 1572868
  247.2 66.1 %reduce-scatter.10.cloned.1.call-start = ((), (), s32[]{:S(2)}) async-start(), calls=%async_computation.12 | async-start | bytes 2621440 | tf_op jit(solution)/shard_map/reduce_scatter | solution.py:61
  273.1 79.7 %all-gather.21.cloned.1.call-start = ((), (), s32[]{:S(2)}) async-start(), calls=%async_computation.17 | async-start | bytes 2621440 | tf_op jit(solution)/shard_map/all_gather | solution.py:103
  328.8 49.0 %all-gather.27.cloned.1.call-start = ((), (), s32[]{:S(2)}) async-start(), calls=%async_computation.23 | async-start | bytes 2621440 | tf_op jit(solution)/shard_map/all_gather | solution.py:67
  328.9 10.8 %copy-start.46 = (bf16[8,128,256]{2,1,0:T(8,128)(2,1)S(1)}, bf16[8,128,256]{2,1,0:T(8,128)(2,1)}, u32[]{:S(2)}) copy-start(bf16[8,128,256]{2,1,0:T(8,128)(2,1)} %get-tuple-element.142) | copy-start | bytes 1572868
  332.0 70.8 %all-gather.17.cloned.1.call-start = ((), (), s32[]{:S(2)}) async-start(), calls=%async_computation.13 | async-start | bytes 2621440 | tf_op jit(solution)/shard_map/all_gather | solution.py:103
  332.8 94.3 %all-gather.23.cloned.1.call-start = ((), (), s32[]{:S(2)}) async-start(), calls=%async_computation.19 | async-start | bytes 2621440 | tf_op jit(solution)/shard_map/all_gather | solution.py:67
  333.4 127.8 %reduce-scatter.22.cloned.1.call-start = ((), (), s32[]{:S(2)}) async-start(), calls=%async_computation.24 | async-start | bytes 2621440 | tf_op jit(solution)/shard_map/reduce_scatter | solution.py:107
  344.3 92.1 %copy-start.81 = (bf16[8,128,256]{2,1,0:T(8,128)(2,1)}, bf16[8,128,256]{2,1,0:T(8,128)(2,1)S(1)}, u32[]{:S(2)}) copy-start(bf16[8,128,256]{2,1,0:T(8,128)(2,1)S(1)} %broadcast_select_fusion) | copy-start | bytes 1572868
  352.8 25.0 %copy-start.82 = (bf16[8,128,256]{2,1,0:T(8,128)(2,1)S(1)}, bf16[8,128,256]{2,1,0:T(8,128)(2,1)}, u32[]{:S(2)}) copy-start(bf16[8,128,256]{2,1,0:T(8,128)(2,1)} %broadcast_select_fusion.1) | copy-start | bytes 1572868
  386.8 108.3 %reduce-scatter.18.cloned.1.call-start = ((), (), s32[]{:S(2)}) async-start(), calls=%async_computation.20 | async-start | bytes 2621440 | tf_op jit(solution)/shard_map/reduce_scatter | solution.py:107
  436.1 93.0 %reduce-scatter.16.cloned.1.call-start = ((), (), s32[]{:S(2)}) async-start(), calls=%async_computation.18 | async-start | bytes 2621440 | tf_op jit(solution)/shard_map/reduce_scatter | solution.py:61
  441.1 54.0 %copy-start.9 = (bf16[1024,256]{1,0:T(8,128)(2,1)S(1)}, bf16[1024,256]{1,0:T(8,128)(2,1)}, u32[]{:S(2)}) copy-start(bf16[1024,256]{1,0:T(8,128)(2,1)} %reduce-scatter.14.cloned.1.call-done) | copy-start | bytes 1572868
  441.1 54.0 %copy-start.10 = (bf16[1024,256]{1,0:T(8,128)(2,1)S(1)}, bf16[1024,256]{1,0:T(8,128)(2,1)}, u32[]{:S(2)}) copy-start(bf16[1024,256]{1,0:T(8,128)(2,1)} %reduce-scatter.10.cloned.1.call-done) | copy-start | bytes 1572868
  441.1 122.0 %reduce-scatter.12.cloned.1.call-start = ((), (), s32[]{:S(2)}) async-start(), calls=%async_computation.14 | async-start | bytes 2621440 | tf_op jit(solution)/shard_map/reduce_scatter | solution.py:61
  446.0 144.4 %all-gather.29.cloned.1.call-start = ((), (), s32[]{:S(2)}) async-start(), calls=%async_computation.25 | async-start | bytes 2621440 | tf_op jit(solution)/shard_map/all_gather | solution.py:67
  453.8 113.7 %copy-start.132 = (s32[8]{0:T(128)}, s32[8]{0:T(128)S(1)}, u32[]{:S(2)}) copy-start(s32[8]{0:T(128)S(1)} %get-tuple-element.38) | copy-start | bytes 100
  457.6 40.4 %copy-start.140 = (s32[8]{0:T(128)}, s32[8]{0:T(128)S(1)}, u32[]{:S(2)}) copy-start(s32[8]{0:T(128)S(1)} %get-tuple-element.34) | copy-start | bytes 100
  567.4 64.6 %all-gather.25.cloned.1.call-start = ((), (), s32[]{:S(2)}) async-start(), calls=%async_computation.21 | async-start | bytes 2621440 | tf_op jit(solution)/shard_map/all_gather | solution.py:67
  573.7 19.8 %copy-start.24 = (bf16[1024,1,256]{0,2,1:T(8,128)(2,1)S(1)}, bf16[1024,1,256]{0,2,1:T(8,128)(2,1)}, u32[]{:S(2)}) copy-start(bf16[1024,1,256]{0,2,1:T(8,128)(2,1)} %slice.799) | copy-start | bytes 1572868
  573.7 223.9 %reduce-scatter.24.cloned.1.call-start = ((), (), s32[]{:S(2)}) async-start(), calls=%async_computation.26 | async-start | bytes 2621440 | tf_op jit(solution)/shard_map/reduce_scatter | solution.py:107
  598.1 14.9 %slice-start.4 = ((s8[8388608]{0:T(1024)(128)(4,1)}), s8[4194304]{0:T(1024)(128)(4,1)S(1)}, s32[]{:S(2)}) async-start(s8[8388608]{0:T(1024)(128)(4,1)} %bitcast.345), calls=%async_computation.32 | async-start | bytes 8388608
  598.1 14.9 %slice-start.6 = ((s8[8388608]{0:T(1024)(128)(4,1)}), s8[4194304]{0:T(1024)(128)(4,1)S(1)}, s32[]{:S(2)}) async-start(s8[8388608]{0:T(1024)(128)(4,1)} %bitcast.347), calls=%async_computation.34 | async-start | bytes 8388608
  598.1 15.6 %slice-start.5 = ((s8[8388608]{0:T(1024)(128)(4,1)}), s8[4194304]{0:T(1024)(128)(4,1)S(1)}, s32[]{:S(2)}) async-start(s8[8388608]{0:T(1024)(128)(4,1)} %bitcast.345), calls=%async_computation.33 | async-start | bytes 8388608
  598.1 17.1 %slice-start.7 = ((s8[8388608]{0:T(1024)(128)(4,1)}), s8[4194304]{0:T(1024)(128)(4,1)S(1)}, s32[]{:S(2)}) async-start(s8[8388608]{0:T(1024)(128)(4,1)} %bitcast.347), calls=%async_computation.35 | async-start | bytes 8388608
  639.7 14.1 %slice-start = ((s8[8388608]{0:T(1024)(128)(4,1)}), s8[4194304]{0:T(1024)(128)(4,1)S(1)}, s32[]{:S(2)}) async-start(s8[8388608]{0:T(1024)(128)(4,1)} %bitcast.341), calls=%async_computation.28 | async-start | bytes 8388608
  639.7 14.1 %slice-start.2 = ((s8[8388608]{0:T(1024)(128)(4,1)}), s8[4194304]{0:T(1024)(128)(4,1)S(1)}, s32[]{:S(2)}) async-start(s8[8388608]{0:T(1024)(128)(4,1)} %bitcast.343), calls=%async_computation.30 | async-start | bytes 8388608
  639.7 15.2 %slice-start.1 = ((s8[8388608]{0:T(1024)(128)(4,1)}), s8[4194304]{0:T(1024)(128)(4,1)S(1)}, s32[]{:S(2)}) async-start(s8[8388608]{0:T(1024)(128)(4,1)} %bitcast.341), calls=%async_computation.29 | async-start | bytes 8388608
  639.8 16.4 %slice-start.3 = ((s8[8388608]{0:T(1024)(128)(4,1)}), s8[4194304]{0:T(1024)(128)(4,1)S(1)}, s32[]{:S(2)}) async-start(s8[8388608]{0:T(1024)(128)(4,1)} %bitcast.343), calls=%async_computation.31 | async-start | bytes 8388608
  733.9 65.8 %reduce-scatter.20.cloned.1.call-start = ((), (), s32[]{:S(2)}) async-start(), calls=%async_computation.22 | async-start | bytes 2621440 | tf_op jit(solution)/shard_map/reduce_scatter | solution.py:107
  766.7 275.1 %reduce-scatter.26.cloned.1.call-start = ((), (), s32[]{:S(2)}) async-start(), calls=%async_computation.27 | async-start | bytes 8257536 | tf_op jit(solution)/shard_map/reduce_scatter | solution.py:55
  788.6 11.0 %copy-start.96 = (f32[1024]{0:T(1024)S(1)}, f32[1024]{0:T(1024)}, u32[]{:S(2)}) copy-start(f32[1024]{0:T(1024)} %copy-done.95) | copy-start | bytes 12292
  788.7 11.0 %copy-start.98 = (f32[1024]{0:T(1024)S(1)}, f32[1024]{0:T(1024)}, u32[]{:S(2)}) copy-start(f32[1024]{0:T(1024)} %copy-done.97) | copy-start | bytes 12292
  788.7 11.0 %copy-start.102 = (f32[1024]{0:T(1024)S(1)}, f32[1024]{0:T(1024)}, u32[]{:S(2)}) copy-start(f32[1024]{0:T(1024)} %copy-done.101) | copy-start | bytes 12292
  788.7 11.0 %copy-start.104 = (f32[1024]{0:T(1024)S(1)}, f32[1024]{0:T(1024)}, u32[]{:S(2)}) copy-start(f32[1024]{0:T(1024)} %copy-done.103) | copy-start | bytes 12292
  788.7 11.0 %copy-start.106 = (f32[1,1,256]{2,0,1:T(1,128)S(1)}, f32[1,1,256]{2,0,1:T(1,128)}, u32[]{:S(2)}) copy-start(f32[1,1,256]{2,0,1:T(1,128)} %copy-done.105) | copy-start | bytes 3076
  788.7 11.0 %copy-start.108 = (f32[1,1,256]{2,0,1:T(1,128)S(1)}, f32[1,1,256]{2,0,1:T(1,128)}, u32[]{:S(2)}) copy-start(f32[1,1,256]{2,0,1:T(1,128)} %copy-done.107) | copy-start | bytes 3076
  788.7 23.7 %copy-start.11 = (bf16[1024,256]{1,0:T(8,128)(2,1)S(1)}, bf16[1024,256]{1,0:T(8,128)(2,1)}, u32[]{:S(2)}) copy-start(bf16[1024,256]{1,0:T(8,128)(2,1)} %reduce-scatter.10.cloned.1.call-done) | copy-start | bytes 1572868
  802.2 13.5 %copy-start.110 = (bf16[2,1024]{1,0:T(2,128)(2,1)S(1)}, bf16[2,1024]{1,0:T(2,128)(2,1)}, u32[]{:S(2)}) copy-start(bf16[2,1024]{1,0:T(2,128)(2,1)} %copy-done.109) | copy-start | bytes 12292
  862.0 13.6 %copy-start.122 = (pred[8]{0:T(512)(128)(4,1)S(1)}, pred[8]{0:T(512)(128)(4,1)}, u32[]{:S(2)}) copy-start(pred[8]{0:T(512)(128)(4,1)} %compare_and_fusion.8) | copy-start | bytes 28
  866.6 13.5 %copy-start.120 = (pred[8]{0:T(512)(128)(4,1)S(1)}, pred[8]{0:T(512)(128)(4,1)}, u32[]{:S(2)}) copy-start(pred[8]{0:T(512)(128)(4,1)} %compare_and_fusion.9) | copy-start | bytes 28
  871.1 13.4 %copy-start.121 = (pred[8]{0:T(512)(128)(4,1)S(1)}, pred[8]{0:T(512)(128)(4,1)}, u32[]{:S(2)}) copy-start(pred[8]{0:T(512)(128)(4,1)} %compare_and_fusion.10) | copy-start | bytes 28
  907.3 43.8 %copy-start.100 = (f32[13,256]{1,0:T(8,128)S(1)}, f32[13,256]{1,0:T(8,128)}, u32[]{:S(2)}) copy-start(f32[13,256]{1,0:T(8,128)} %param.29) | copy-start | bytes 39940
  907.4 43.8 %copy-start.111 = (f32[13,256]{1,0:T(8,128)S(1)}, f32[13,256]{1,0:T(8,128)}, u32[]{:S(2)}) copy-start(f32[13,256]{1,0:T(8,128)} %param.31) | copy-start | bytes 39940
  907.4 43.8 %copy-start.112 = (f32[13,256]{1,0:T(8,128)S(1)}, f32[13,256]{1,0:T(8,128)}, u32[]{:S(2)}) copy-start(f32[13,256]{1,0:T(8,128)} %param.30) | copy-start | bytes 39940
  953.8 90.3 %copy-start.64 = (f32[128,14,256]{2,0,1:T(8,128)S(1)}, f32[128,14,256]{2,0,1:T(8,128)}, u32[]{:S(2)}) copy-start(f32[128,14,256]{2,0,1:T(8,128)} %param.25) | copy-start | bytes 5505028
  (113 other events, 477.4 us)
Sparse Core Ops, SparseCore 0:
  10.9 63.1 all-gather.10
  76.3 71.9 all-gather.14
  150.5 21.1 all-gather.12
  173.6 22.8 all-gather.18
  247.4 31.3 reduce-scatter.13
  281.9 31.4 reduce-scatter.9
  329.0 23.8 all-gather.20
  354.9 22.8 all-gather.26
  379.9 22.8 all-gather.16
  404.2 22.8 all-gather.22
  429.6 31.4 reduce-scatter.21
  463.7 31.4 reduce-scatter.17
  497.7 31.4 reduce-scatter.15
  531.7 31.3 reduce-scatter.11
  567.5 22.8 all-gather.28
  592.4 22.8 all-gather.24
  734.0 31.5 reduce-scatter.23
  768.2 31.4 reduce-scatter.19
  907.4 134.4 reduce-scatter.25
where the time goes:
time: 1070 us; the launch traced here: 1060 us
  waiting for transfers between devices  413 us (39%)
  matrix products  199 us (19%)
  other arithmetic  186 us (17%)
  local copies, waits for them, and re-layouts  166 us (16%)
  blocking collectives  82.8 us (8%)
  between operations  16.3 us (2%)
    reduce_scatter x4, waiting for transfers between devices, branch_total(): lax.psum_scatter(partial_rows.astype(jnp.bfloat16), 'mp', scatter_dimensi...  93.6 us
    reduce_scatter x1, waiting for transfers between devices, reduce_grads(): lax.psum_scatter(values.astype(jnp.bfloat16), 'dp', scatter_dimension=0,...  85.2 us
    all_gather x4, waiting for transfers between devices, branch_spread(): return lax.all_gather(grad_rows, 'mp', axis=1, tiled=True)  56.9 us
    all_gather x1, waiting for transfers between devices, gather_block(): whole_rows = lax.all_gather(low_weights[:, :8, :], 'dp', axis=0, tiled=True)  48.6 us
    all_gather x1, waiting for transfers between devices, body(): mod_whole = lax.all_gather(low_weights[:, 8:, :], 'dp', axis=0, tiled=True)  47.2 us
    another operation x16, other arithmetic  44.2 us
    all_gather x4, waiting for transfers between devices, modulated(): return (lax.all_gather(low_rows, 'mp', axis=1, tiled=True), normed, inverse)  43.6 us
    psum x1, blocking collectives, body(): bias_grad = lax.psum(bias_local, 'dp')  39.7 us
  transfers between devices with their start and end apart: 19, of which 17 were waited for; matrix products, arithmetic and copies ran while one was open for 25% of the time, Pallas kernels for 0%

commit v1 on v0

--- a/solution.py
+++ b/solution.py
@@ -22,6 +22,28 @@
 masked_score = -1e30
 
 
+def laid_out(tiles, dim):
+    dims = list(tiles.shape[1:])
+    dims[dim] *= tiles.shape[0]
+    return jnp.moveaxis(tiles, 0, dim).reshape(dims)
+
+
+def collect(value, axis, dim):
+    devices = lax.axis_size(axis)
+    pairs = [(i, (i + 1) % devices) for i in range(devices)]
+    back = [(b, a) for a, b in pairs]
+    lower, upper = ([], [])
+    for lap in range(devices - 1):
+        if lap % 2 == 0:
+            lower.append(lax.ppermute(lower[-1] if lower else value, axis, pairs))
+        else:
+            upper.append(lax.ppermute(upper[-1] if upper else value, axis, back))
+    parts = jnp.stack([*lower[::-1], value, *upper])
+    shift = lax.axis_index(axis) - len(lower)
+    parts = parts[(jnp.arange(devices) - shift) % devices]
+    return laid_out(parts, dim)
+
+
 def true_order(gathered, owners):
     block_count = owners.shape[1]
     blocks = gathered.reshape(
@@ -100,7 +122,7 @@
     inverse = lax.rsqrt(spread + norm_epsilon)
     normed = (values - row_mean[:, None]) * inverse[:, None]
     low_rows = (normed * (1.0 + scale_row) + shift_row).astype(jnp.bfloat16)
-    return (lax.all_gather(low_rows, "mp", axis=1, tiled=True), normed, inverse)
+    return (collect(low_rows, "mp", 1), normed, inverse)
 
 
 def norm_back(partial_rows, normed, inverse, scale_row):

time: 1070 us -> 1010 us (0.944)
  waiting for transfers between devices: 413 us -> 308 us
  local copies, waits for them, and re-layouts: 166 us -> 197 us
    ppermute x0 -> x12, waiting for transfers between devices: none -> 59.6 us  [the longest x8 59.6 us: collect(): lower.append(lax.ppermute(lower[-1] if lower else value, axis, pairs))]
    all_gather x1, waiting for transfers between devices: 48.6 us -> 2.86 us  [gather_block(): whole_rows = lax.all_gather(low_weights[:, :8, :], 'dp', axis=0, tiled=True)]
    all_gather x4 -> x0, waiting for transfers between devices: 43.6 us -> none  [modulated(): return (lax.all_gather(low_rows, 'mp', axis=1, tiled=True), normed, inverse)]
    all_gather x4, waiting for transfers between devices: 56.9 us -> 16.4 us  [branch_spread(): return lax.all_gather(grad_rows, 'mp', axis=1, tiled=True)]
    reduce_scatter x4, waiting for transfers between devices: 36.4 us -> 8.3 us  [norm_back(): lax.psum_scatter(partial_rows.astype(jnp.bfloat16), 'mp', scatter_dimensi...]
    transpose x0 -> x4, local copies, waits for them, and re-layouts: none -> 15.9 us  [laid_out(): return jnp.moveaxis(tiles, 0, dim).reshape(dims)]
    gather x0 -> x4, local copies, waits for them, and re-layouts: none -> 14.4 us  [collect(): parts = parts[(jnp.arange(devices) - shift) % devices]]
    another operation x16 -> x20, other arithmetic: 44.2 us -> 54.6 us
  transfers between devices with their start and end apart: 19 -> 27, of which waited for: 17 -> 16; matrix products, arithmetic and copies ran while one was open for 25% -> 28% of each run, Pallas kernels for 0% -> 0%
where the time goes in v1:
time: 1010 us; the launch traced here: 1000 us
  waiting for transfers between devices  308 us (30%)
  matrix products  198 us (20%)
  local copies, waits for them, and re-layouts  197 us (20%)
  other arithmetic  193 us (19%)
  blocking collectives  82.9 us (8%)
  between operations  16.3 us (2%)
    reduce_scatter x4, waiting for transfers between devices, branch_total(): lax.psum_scatter(partial_rows.astype(jnp.bfloat16), 'mp', scatter_dimensi...  87.8 us
    reduce_scatter x1, waiting for transfers between devices, reduce_grads(): lax.psum_scatter(values.astype(jnp.bfloat16), 'dp', scatter_dimension=0,...  86.3 us
    ppermute x8, waiting for transfers between devices, collect(): lower.append(lax.ppermute(lower[-1] if lower else value, axis, pairs))  59.6 us
    all_gather x1, waiting for transfers between devices, body(): mod_whole = lax.all_gather(low_weights[:, 8:, :], 'dp', axis=0, tiled=True)  46.4 us
    another operation x16, other arithmetic  44.5 us
    psum x1, blocking collectives, body(): bias_grad = lax.psum(bias_local, 'dp')  39.8 us
    dot_general x4, matrix products, attend_back(): jnp.einsum('qhd,khd->hqk', grad_rows, values_in, preferred_element_type=j...  37.7 us
    gather x14, local copies, waits for them, and re-layouts, stored_order(): jnp.take(blocks[:, :, slot_index, :], jnp.argsort(owners[slot_index]), ax...  32.5 us
  transfers between devices with their start and end apart: 27, of which 16 were waited for; matrix products, arithmetic and copies ran while one was open for 28% of the time, Pallas kernels for 0%

profile of v1, /device:TPU:0, one launch (start us, length us, event | category | flops | bytes accessed | tf_op | source)
XLA Modules:
  0.0 1004.9 jit_solution(8590390625392238055)
XLA Ops:
  13.8 12.6 %all-reduce.3 = (f32[1024]{0:T(1024)S(1)}, f32[1024]{0:T(1024)S(1)}, f32[1024]{0:T(1024)S(1)}, f32[1024]{0:T(1024)S(1)}) all-reduce(f32[1024]{0:T(1024)S(1)} %get-tuple-element.61, f32[1024]{0:T(1024)S(1)} %get-tuple-element.60, f32[1024]{0:T(1024)S(1)} %get-tuple-element.62, ...), channel_id=1, replica_groups=mesh['dp'=8,'mp'=4] {'mp'}, use_global_device_ids=true, to_apply=%region_3.5 | all-reduce | flops 4096 | bytes 32768 | tf_op jit(solution)/shard_map/psum | solution.py:119
  27.6 46.4 %all-gather.7.cloned.1.call-done = bf16[1024,6,256]{2,0,1:T(8,128)(2,1)} async-done(((bf16[128,6,256]{2,0,1:T(8,128)(2,1)}), bf16[1024,6,256]{2,0,1:T(8,128)(2,1)}) %all-gather.7.cloned.1.call-update) | async-done | bytes 3145744 | tf_op jit(solution)/shard_map/all_gather | solution.py:231
  74.0 3.2 slice_bitcast_fusion.22
  98.1 7.7 collective-permute-done.6
  107.6 9.4 collective-permute-done
  118.7 7.2 collective-permute-done.7
  127.5 3.6 gather_fusion.2
  131.1 4.0 copy.46
  137.9 3.6 gather_fusion
  141.5 3.9 copy.39
  148.3 3.8 slice_bitcast_fusion.17
  163.8 3.7 convolution_add_fusion.1
  185.9 8.7 subtract_convert_fusion.4
  197.8 3.4 fusion.109
  205.5 3.4 exponential_reduce_fusion.1
  227.9 3.4 fusion.110
  235.7 3.4 exponential_reduce_fusion.3
  254.5 32.8 %reduce-scatter.10.cloned.1.call-done = bf16[1024,256]{1,0:T(8,128)(2,1)} async-done(((bf16[1024,1024]{1,0:T(8,128)(2,1)}), bf16[1024,256]{1,0:T(8,128)(2,1)}) %reduce-scatter.10.cloned.1.call-update) | async-done | bytes 524304 | tf_op jit(solution)/shard_map/reduce_scatter | solution.py:83
  289.6 10.2 %all-reduce.2 = (f32[1024]{0:T(1024)S(1)}, f32[1024]{0:T(1024)S(1)}, f32[1024]{0:T(1024)S(1)}, f32[1024]{0:T(1024)S(1)}) all-reduce(f32[1024]{0:T(1024)S(1)} %get-tuple-element.56, f32[1024]{0:T(1024)S(1)} %get-tuple-element.57, f32[1024]{0:T(1024)S(1)} %get-tuple-element.49, ...), channel_id=1, replica_groups=mesh['dp'=8,'mp'=4] {'mp'}, use_global_device_ids=true, to_apply=%region_26.28 | all-reduce | flops 4096 | bytes 32768 | tf_op jit(solution)/shard_map/psum | solution.py:119
  310.6 6.5 collective-permute-done.9
  332.6 3.7 gather_fusion.3
  336.2 4.0 copy.48
  340.2 4.4 fusion.164
  344.6 5.7 convert_reduce_fusion.2
  355.8 12.0 %collective-permute-done.3 = bf16[1024,256]{1,0:T(8,128)(2,1)S(1)} collective-permute-done((bf16[1024,256]{1,0:T(8,128)(2,1)}, bf16[1024,256]{1,0:T(8,128)(2,1)S(1)}, u32[]{:S(2)}, u32[]{:S(2)}) %collective-permute-start.3) | collective-permute-done | bytes 524320 | tf_op jit(solution)/shard_map/ppermute | solution.py:38
  368.0 15.1 %collective-permute-done.4 = bf16[1024,256]{1,0:T(8,128)(2,1)S(1)} collective-permute-done((bf16[1024,256]{1,0:T(8,128)(2,1)S(1)}, bf16[1024,256]{1,0:T(8,128)(2,1)S(1)}, u32[]{:S(2)}, u32[]{:S(2)}) %collective-permute-start.4) | collective-permute-done | bytes 524320 | tf_op jit(solution)/shard_map/ppermute | solution.py:38
  385.8 3.6 gather_fusion.1
  389.4 4.0 copy.44
  393.4 4.4 fusion.165
  397.8 5.7 convert_reduce_fusion.3
  407.2 4.7 bitcast_convert_fusion.4
  411.9 4.7 bitcast_convert_fusion.5
  431.6 7.1 reduce-scatter.18.cloned.1.call-done
  441.5 10.1 %all-reduce.1 = (f32[1024]{0:T(1024)S(1)}, f32[1024]{0:T(1024)S(1)}, f32[1024]{0:T(1024)S(1)}, f32[1024]{0:T(1024)S(1)}) all-reduce(f32[1024]{0:T(1024)S(1)} %get-tuple-element.54, f32[1024]{0:T(1024)S(1)} %get-tuple-element.66, f32[1024]{0:T(1024)S(1)} %get-tuple-element.41, ...), channel_id=1, replica_groups=mesh['dp'=8,'mp'=4] {'mp'}, use_global_device_ids=true, to_apply=%region_44.46 | all-reduce | flops 4096 | bytes 32768 | tf_op jit(solution)/shard_map/psum | solution.py:133
  451.6 20.9 %reduce-scatter.16.cloned.1.call-done = bf16[1024,256]{1,0:T(8,128)(2,1)} async-done(((bf16[1024,1024]{1,0:T(8,128)(2,1)}), bf16[1024,256]{1,0:T(8,128)(2,1)}) %reduce-scatter.16.cloned.1.call-update) | async-done | bytes 524304 | tf_op jit(solution)/shard_map/reduce_scatter | solution.py:83
  472.6 34.0 %reduce-scatter.12.cloned.1.call-done = bf16[1024,256]{1,0:T(8,128)(2,1)} async-done(((bf16[1024,1024]{1,0:T(8,128)(2,1)}), bf16[1024,256]{1,0:T(8,128)(2,1)}) %reduce-scatter.12.cloned.1.call-update) | async-done | bytes 524304 | tf_op jit(solution)/shard_map/reduce_scatter | solution.py:83
  506.6 4.2 convert_reduce_fusion.11
  513.1 3.9 convert_reduce_fusion.13
  517.5 16.4 %all-gather.17.cloned.1.call-done = bf16[1024,1024]{1,0:T(8,128)(2,1)} async-done(((bf16[1024,256]{1,0:T(8,128)(2,1)}), bf16[1024,1024]{1,0:T(8,128)(2,1)}) %all-gather.17.cloned.1.call-update) | async-done | bytes 2097168 | tf_op jit(solution)/shard_map/all_gather | solution.py:89
  537.0 4.5 fusion.183
  541.5 14.6 %multiply_reduce_fusion = (f32[4,512]{1,0:T(4,128)S(1)}, f32[4,512]{1,0:T(4,128)S(1)}, f32[4,512,1024]{2,1,0:T(8,128)}) fusion(f32[4,512,1024]{2,1,0:T(8,128)} %copy-done.3, f32[4,512]{1,0:T(4,128)S(1)} %log_add_fusion, pred[1024]{0:T(1024)(128)(4,1)S(1)} %iota_compare_fusion, f32[4,512,1024]{2,1,0:T(8,128)} %fusion.183, f32[4,512]{1,0:T(4,128)S(1)} %log_add_fusion.1, ...), kind=kOutput, calls=%fused_computation.35 | convolution fusion | flops 289402880 | bytes 34374656 | tf_op jit(solution)/shard_map/qhd,khd->hqk/dot_general | solution.py:187
  558.5 9.9 multiply_convert_fusion
  578.5 4.5 fusion.181
  583.0 14.1 %multiply_reduce_fusion.2 = (f32[4,512]{1,0:T(4,128)S(1)}, f32[4,512]{1,0:T(4,128)S(1)}, f32[4,512,1024]{2,1,0:T(8,128)}) fusion(f32[4,512,1024]{2,1,0:T(8,128)} %copy-done.2, f32[4,512]{1,0:T(4,128)S(1)} %log_add_fusion.2, pred[1024]{0:T(1024)(128)(4,1)S(1)} %iota_compare_fusion.1, f32[4,512,1024]{2,1,0:T(8,128)} %fusion.181, ...), kind=kOutput, calls=%fused_computation.39 | convolution fusion | flops 289402880 | bytes 34374656 | tf_op jit(solution)/shard_map/qhd,khd->hqk/dot_general | solution.py:187
  599.4 10.1 %multiply_convert_fusion.2 = (bf16[4,512,1024]{2,1,0:T(8,128)(2,1)}, bf16[4,512,1024]{2,1,0:T(8,128)(2,1)S(1)}) fusion(f32[4,512,1024]{2,1,0:T(8,128)} %get-tuple-element.243, f32[4,512,1024]{2,1,0:T(8,128)S(1)} %bitcast.362, f32[4,512]{1,0:T(4,128)S(1)} %get-tuple-element.88, f32[4,512]{1,0:T(4,128)S(1)} %log_add_fusion.2, ...), kind=kLoop, calls=%fused_computation.38 | loop fusion | flops 25165824 | bytes 41976832 | tf_op jit(solution)/shard_map/convert_element_type | solution.py:191
  613.5 6.1 fusion.66
  621.8 4.5 fusion.70
  636.2 4.5 fusion.68
  650.4 8.5 subtract_convert_fusion.3
  672.1 5.0 bitcast_convert_fusion
  677.8 5.4 fusion.120
  683.2 6.7 fusion.65
  706.1 4.9 bitcast_convert_fusion.2
  711.5 4.5 fusion.186
  733.1 8.7 maximum_add_fusion
  745.5 10.1 %all-reduce = (f32[1024]{0:T(1024)S(1)}, f32[1024]{0:T(1024)S(1)}, f32[1024]{0:T(1024)S(1)}, f32[1024]{0:T(1024)S(1)}) all-reduce(f32[1024]{0:T(1024)S(1)} %get-tuple-element.58, f32[1024]{0:T(1024)S(1)} %get-tuple-element.64, f32[1024]{0:T(1024)S(1)} %get-tuple-element.45, ...), channel_id=1, replica_groups=mesh['dp'=8,'mp'=4] {'mp'}, use_global_device_ids=true, to_apply=%region_51.53 | all-reduce | flops 4096 | bytes 32768 | tf_op jit(solution)/shard_map/psum | solution.py:133
  755.7 3.2 multiply_reduce_fusion.5
  759.0 4.1 fusion.124
  763.1 6.7 pad_maximum_fusion
  769.9 5.8 slice_bitcast_fusion
  850.5 39.8 %psum.135 = f32[13,256]{1,0:T(8,128)S(1)} all-reduce(f32[13,256]{1,0:T(8,128)S(1)} %pad_maximum_fusion.28), channel_id=1, replica_groups=mesh['dp'=8,'mp'=4] {'dp'}, use_global_device_ids=true, to_apply=%region_87.90 | all-reduce | flops 3328 | bytes 26624 | tf_op jit(solution)/shard_map/psum | solution.py:384
  895.6 86.3 %reduce-scatter.26.cloned.1.call-done = bf16[128,14,256]{2,0,1:T(8,128)(2,1)} async-done(((bf16[1024,14,256]{2,0,1:T(8,128)(2,1)}), bf16[128,14,256]{2,0,1:T(8,128)(2,1)}) %reduce-scatter.26.cloned.1.call-update) | async-done | bytes 917520 | tf_op jit(solution)/shard_map/reduce_scatter | solution.py:77
  984.2 4.3 fusion.30
  991.4 5.4 fusion.180
  (678 shorter events, 356.7 us)
Async XLA Ops:
  7.2 974.7 %copy-start = (f32[14,128,128]{2,1,0:T(8,128)S(1)}, f32[14,128,128]{2,1,0:T(8,128)}, u32[]{:S(2)}) copy-start(f32[14,128,128]{2,1,0:T(8,128)} %param.27) | copy-start | bytes 2752516
  7.2 66.8 %all-gather.7.cloned.1.call-start = ((), (), s32[]{:S(2)}) async-start(), calls=%async_computation.9 | async-start | bytes 3538944 | tf_op jit(solution)/shard_map/all_gather | solution.py:231
  9.9 16.7 %copy-start.126 = (s32[2]{0:T(128)S(1)}, s32[2]{0:T(128)}, u32[]{:S(2)}) copy-start(s32[2]{0:T(128)} %param.20) | copy-start | bytes 28
  9.9 17.5 %copy-start.134 = (f32[8,1024]{1,0:T(8,128)S(1)}, f32[8,1024]{1,0:T(8,128)}, u32[]{:S(2)}) copy-start(f32[8,1024]{1,0:T(8,128)} %param.22) | copy-start | bytes 98308
  9.9 17.5 %copy-start.135 = (s32[2]{0:T(128)S(1)}, s32[2]{0:T(128)}, u32[]{:S(2)}) copy-start(s32[2]{0:T(128)} %param.21) | copy-start | bytes 28
  10.7 137.6 %all-gather.9.cloned.1.call-start = ((), (), s32[]{:S(2)}) async-start(), calls=%async_computation.10 | async-start | bytes 4718592 | tf_op jit(solution)/shard_map/all_gather | solution.py:72
  12.6 241.8 %reduce-scatter.14.cloned.1.call-start = ((), (), s32[]{:S(2)}) async-start(), calls=%async_computation.13 | async-start | bytes 2621440 | tf_op jit(solution)/shard_map/reduce_scatter | solution.py:83
  27.3 66.5 %copy-start.102 = (f32[1024]{0:T(1024)}, f32[1024]{0:T(1024)S(1)}, u32[]{:S(2)}) copy-start(f32[1024]{0:T(1024)S(1)} %get-tuple-element.293) | copy-start | bytes 12292
  27.3 66.5 %copy-start.104 = (f32[1024]{0:T(1024)}, f32[1024]{0:T(1024)S(1)}, u32[]{:S(2)}) copy-start(f32[1024]{0:T(1024)S(1)} %get-tuple-element.294) | copy-start | bytes 12292
  27.4 66.5 %copy-start.108 = (f32[1024]{0:T(1024)}, f32[1024]{0:T(1024)S(1)}, u32[]{:S(2)}) copy-start(f32[1024]{0:T(1024)S(1)} %get-tuple-element.224) | copy-start | bytes 12292
  27.4 66.5 %copy-start.110 = (f32[1024]{0:T(1024)}, f32[1024]{0:T(1024)S(1)}, u32[]{:S(2)}) copy-start(f32[1024]{0:T(1024)S(1)} %get-tuple-element.225) | copy-start | bytes 12292
  27.6 65.7 %copy-start.116 = (bf16[2,1024]{1,0:T(2,128)(2,1)}, bf16[2,1024]{1,0:T(2,128)(2,1)S(1)}, u32[]{:S(2)}) copy-start(bf16[2,1024]{1,0:T(2,128)(2,1)S(1)} %fusion.128) | copy-start | bytes 12292
  93.8 33.6 %copy-start.112 = (f32[1,1,256]{2,0,1:T(1,128)}, f32[1,1,256]{2,0,1:T(1,128)S(1)}, u32[]{:S(2)}) copy-start(f32[1,1,256]{2,0,1:T(1,128)S(1)} %get-tuple-element.218) | copy-start | bytes 3076
  93.9 33.6 %copy-start.114 = (f32[1,1,256]{2,0,1:T(1,128)}, f32[1,1,256]{2,0,1:T(1,128)S(1)}, u32[]{:S(2)}) copy-start(f32[1,1,256]{2,0,1:T(1,128)S(1)} %get-tuple-element.213) | copy-start | bytes 3076
  94.8 11.0 %collective-permute-start.6 = (bf16[1024,256]{1,0:T(8,128)(2,1)S(1)}, bf16[1024,256]{1,0:T(8,128)(2,1)S(1)}, u32[]{:S(2)}, u32[]{:S(2)}) collective-permute-start(bf16[1024,256]{1,0:T(8,128)(2,1)S(1)} %get-tuple-element.186), channel_id=1, source_target_pairs={{0,1},{1,2},{2,3},{3,0},{4,5},{5,6},{6,7},{7,4},{8,9},{9,10},{10,1... | collective-permute-start | bytes 1572872 | tf_op jit(solution)/shard_map/ppermute | solution.py:38
  95.5 21.5 %collective-permute-start = (bf16[1024,256]{1,0:T(8,128)(2,1)S(1)}, bf16[1024,256]{1,0:T(8,128)(2,1)S(1)}, u32[]{:S(2)}, u32[]{:S(2)}) collective-permute-start(bf16[1024,256]{1,0:T(8,128)(2,1)S(1)} %get-tuple-element.187), channel_id=1, source_target_pairs={{0,1},{1,2},{2,3},{3,0},{4,5},{5,6},{6,7},{7,4},{8,9},{9,10},{10,1... | collective-permute-start | bytes 1572872 | tf_op jit(solution)/shard_map/ppermute | solution.py:38
  97.8 20.8 %collective-permute-start.8 = (bf16[1024,256]{1,0:T(8,128)(2,1)S(1)}, bf16[1024,256]{1,0:T(8,128)(2,1)S(1)}, u32[]{:S(2)}, u32[]{:S(2)}) collective-permute-start(bf16[1024,256]{1,0:T(8,128)(2,1)S(1)} %get-tuple-element.186), channel_id=1, source_target_pairs={{1,0},{2,1},{3,2},{0,3},{5,4},{6,5},{7,6},{4,7},{9,8},{10,9},{11,1... | collective-permute-start | bytes 1572872 | tf_op jit(solution)/shard_map/ppermute | solution.py:40
  105.8 20.2 %collective-permute-start.7 = (bf16[1024,256]{1,0:T(8,128)(2,1)S(1)}, bf16[1024,256]{1,0:T(8,128)(2,1)S(1)}, u32[]{:S(2)}, u32[]{:S(2)}) collective-permute-start(bf16[1024,256]{1,0:T(8,128)(2,1)S(1)} %collective-permute-done.6), channel_id=1, source_target_pairs={{0,1},{1,2},{2,3},{3,0},{4,5},{5,6},{6,7},{7,4},{8,9},{9,10},{10,1... | collective-permute-start | bytes 1572872 | tf_op jit(solution)/shard_map/ppermute | solution.py:38
  105.8 29.3 %collective-permute-start.2 = (bf16[1024,256]{1,0:T(8,128)(2,1)S(1)}, bf16[1024,256]{1,0:T(8,128)(2,1)}, u32[]{:S(2)}, u32[]{:S(2)}) collective-permute-start(bf16[1024,256]{1,0:T(8,128)(2,1)S(1)} %get-tuple-element.187), channel_id=1, source_target_pairs={{1,0},{2,1},{3,2},{0,3},{5,4},{6,5},{7,6},{4,7},{9,8},{10,9},{11,1... | collective-permute-start | bytes 1572872 | tf_op jit(solution)/shard_map/ppermute | solution.py:40
  117.0 18.1 %collective-permute-start.1 = (bf16[1024,256]{1,0:T(8,128)(2,1)S(1)}, bf16[1024,256]{1,0:T(8,128)(2,1)}, u32[]{:S(2)}, u32[]{:S(2)}) collective-permute-start(bf16[1024,256]{1,0:T(8,128)(2,1)S(1)} %collective-permute-done), channel_id=1, source_target_pairs={{0,1},{1,2},{2,3},{3,0},{4,5},{5,6},{6,7},{7,4},{8,9},{9,10},{10,1... | collective-permute-start | bytes 1572872 | tf_op jit(solution)/shard_map/ppermute | solution.py:38
  118.7 67.3 %copy-start.78 = (f32[1024,32]{0,1:T(8,128)}, f32[1024,32]{0,1:T(8,128)S(1)}, u32[]{:S(2)}) copy-start(f32[1024,32]{0,1:T(8,128)S(1)} %get-tuple-element.234) | copy-start | bytes 393220
  167.6 76.8 %copy-start.21 = (bf16[1024,1,256]{0,2,1:T(8,128)(2,1)}, bf16[1024,1,256]{0,2,1:T(8,128)(2,1)S(1)}, u32[]{:S(2)}) copy-start(bf16[1024,1,256]{0,2,1:T(8,128)(2,1)S(1)} %slice.808) | copy-start | bytes 1572868
  223.4 63.9 %reduce-scatter.10.cloned.1.call-start = ((), (), s32[]{:S(2)}) async-start(), calls=%async_computation.11 | async-start | bytes 2621440 | tf_op jit(solution)/shard_map/reduce_scatter | solution.py:83
  249.4 95.2 %all-gather.15.cloned.1.call-start = ((), (), s32[]{:S(2)}) async-start(), calls=%async_computation.19 | async-start | bytes 2621440 | tf_op jit(solution)/shard_map/all_gather | solution.py:89
  252.5 145.3 %all-gather.11.cloned.1.call-start = ((), (), s32[]{:S(2)}) async-start(), calls=%async_computation.15 | async-start | bytes 2621440 | tf_op jit(solution)/shard_map/all_gather | solution.py:89
  254.0 177.6 %reduce-scatter.22.cloned.1.call-start = ((), (), s32[]{:S(2)}) async-start(), calls=%async_computation.20 | async-start | bytes 2621440 | tf_op jit(solution)/shard_map/reduce_scatter | solution.py:129
  254.4 45.3 %copy-start.9 = (bf16[1024,256]{1,0:T(8,128)(2,1)S(1)}, bf16[1024,256]{1,0:T(8,128)(2,1)}, u32[]{:S(2)}) copy-start(bf16[1024,256]{1,0:T(8,128)(2,1)} %reduce-scatter.14.cloned.1.call-done) | copy-start | bytes 1572868
  287.3 12.5 %copy-start.10 = (bf16[1024,256]{1,0:T(8,128)(2,1)S(1)}, bf16[1024,256]{1,0:T(8,128)(2,1)}, u32[]{:S(2)}) copy-start(bf16[1024,256]{1,0:T(8,128)(2,1)} %reduce-scatter.10.cloned.1.call-done) | copy-start | bytes 1572868
  302.0 15.0 %collective-permute-start.9 = (bf16[1024,256]{1,0:T(8,128)(2,1)}, bf16[1024,256]{1,0:T(8,128)(2,1)}, u32[]{:S(2)}, u32[]{:S(2)}) collective-permute-start(bf16[1024,256]{1,0:T(8,128)(2,1)} %get-tuple-element.180), channel_id=1, source_target_pairs={{0,1},{1,2},{2,3},{3,0},{4,5},{5,6},{6,7},{7,4},{8,9},{9,10},{10,1... | collective-permute-start | bytes 1572872 | tf_op jit(solution)/shard_map/ppermute | solution.py:38
  308.8 19.0 %collective-permute-start.11 = (bf16[1024,256]{1,0:T(8,128)(2,1)}, bf16[1024,256]{1,0:T(8,128)(2,1)}, u32[]{:S(2)}, u32[]{:S(2)}) collective-permute-start(bf16[1024,256]{1,0:T(8,128)(2,1)} %get-tuple-element.180), channel_id=1, source_target_pairs={{1,0},{2,1},{3,2},{0,3},{5,4},{6,5},{7,6},{4,7},{9,8},{10,9},{11,1... | collective-permute-start | bytes 1572872 | tf_op jit(solution)/shard_map/ppermute | solution.py:40
  317.0 12.4 %collective-permute-start.10 = (bf16[1024,256]{1,0:T(8,128)(2,1)}, bf16[1024,256]{1,0:T(8,128)(2,1)}, u32[]{:S(2)}, u32[]{:S(2)}) collective-permute-start(bf16[1024,256]{1,0:T(8,128)(2,1)} %collective-permute-done.9), channel_id=1, source_target_pairs={{0,1},{1,2},{2,3},{3,0},{4,5},{5,6},{6,7},{7,4},{8,9},{9,10},{10,1... | collective-permute-start | bytes 1572872 | tf_op jit(solution)/shard_map/ppermute | solution.py:38
  354.0 84.7 %reduce-scatter.18.cloned.1.call-start = ((), (), s32[]{:S(2)}) async-start(), calls=%async_computation.16 | async-start | bytes 2621440 | tf_op jit(solution)/shard_map/reduce_scatter | solution.py:129
  354.0 13.8 %collective-permute-start.3 = (bf16[1024,256]{1,0:T(8,128)(2,1)}, bf16[1024,256]{1,0:T(8,128)(2,1)S(1)}, u32[]{:S(2)}, u32[]{:S(2)}) collective-permute-start(bf16[1024,256]{1,0:T(8,128)(2,1)} %get-tuple-element.179), channel_id=1, source_target_pairs={{0,1},{1,2},{2,3},{3,0},{4,5},{5,6},{6,7},{7,4},{8,9},{9,10},{10,1... | collective-permute-start | bytes 1572872 | tf_op jit(solution)/shard_map/ppermute | solution.py:38
  354.1 13.9 %collective-permute-start.5 = (bf16[1024,256]{1,0:T(8,128)(2,1)}, bf16[1024,256]{1,0:T(8,128)(2,1)S(1)}, u32[]{:S(2)}, u32[]{:S(2)}) collective-permute-start(bf16[1024,256]{1,0:T(8,128)(2,1)} %get-tuple-element.179), channel_id=1, source_target_pairs={{1,0},{2,1},{3,2},{0,3},{5,4},{6,5},{7,6},{4,7},{9,8},{10,9},{11,1... | collective-permute-start | bytes 1572872 | tf_op jit(solution)/shard_map/ppermute | solution.py:40
  367.8 15.3 %collective-permute-start.4 = (bf16[1024,256]{1,0:T(8,128)(2,1)S(1)}, bf16[1024,256]{1,0:T(8,128)(2,1)S(1)}, u32[]{:S(2)}, u32[]{:S(2)}) collective-permute-start(bf16[1024,256]{1,0:T(8,128)(2,1)S(1)} %collective-permute-done.3), channel_id=1, source_target_pairs={{0,1},{1,2},{2,3},{3,0},{4,5},{5,6},{6,7},{7,4},{8,9},{9,10},{10,1... | collective-permute-start | bytes 1572872 | tf_op jit(solution)/shard_map/ppermute | solution.py:38
  407.2 65.4 %reduce-scatter.16.cloned.1.call-start = ((), (), s32[]{:S(2)}) async-start(), calls=%async_computation.14 | async-start | bytes 2621440 | tf_op jit(solution)/shard_map/reduce_scatter | solution.py:83
  411.9 94.7 %reduce-scatter.12.cloned.1.call-start = ((), (), s32[]{:S(2)}) async-start(), calls=%async_computation.12 | async-start | bytes 2621440 | tf_op jit(solution)/shard_map/reduce_scatter | solution.py:83
  416.7 117.1 %all-gather.17.cloned.1.call-start = ((), (), s32[]{:S(2)}) async-start(), calls=%async_computation.21 | async-start | bytes 2621440 | tf_op jit(solution)/shard_map/all_gather | solution.py:89
  424.5 86.4 %copy-start.136 = (s32[8]{0:T(128)}, s32[8]{0:T(128)S(1)}, u32[]{:S(2)}) copy-start(s32[8]{0:T(128)S(1)} %get-tuple-element.38) | copy-start | bytes 100
  425.4 16.0 %copy-start.138 = (s32[8]{0:T(128)}, s32[8]{0:T(128)S(1)}, u32[]{:S(2)}) copy-start(s32[8]{0:T(128)S(1)} %get-tuple-element.37) | copy-start | bytes 100
  428.4 13.1 %copy-start.144 = (s32[8]{0:T(128)}, s32[8]{0:T(128)S(1)}, u32[]{:S(2)}) copy-start(s32[8]{0:T(128)S(1)} %get-tuple-element.34) | copy-start | bytes 100
  510.8 64.5 %all-gather.13.cloned.1.call-start = ((), (), s32[]{:S(2)}) async-start(), calls=%async_computation.17 | async-start | bytes 2621440 | tf_op jit(solution)/shard_map/all_gather | solution.py:89
  517.0 20.0 %copy-start.24 = (bf16[1024,1,256]{0,2,1:T(8,128)(2,1)S(1)}, bf16[1024,1,256]{0,2,1:T(8,128)(2,1)}, u32[]{:S(2)}) copy-start(bf16[1024,1,256]{0,2,1:T(8,128)(2,1)} %slice.807) | copy-start | bytes 1572868
  517.0 224.7 %reduce-scatter.24.cloned.1.call-start = ((), (), s32[]{:S(2)}) async-start(), calls=%async_computation.22 | async-start | bytes 2621440 | tf_op jit(solution)/shard_map/reduce_scatter | solution.py:129
  541.5 14.6 %slice-start.4 = ((s8[8388608]{0:T(1024)(128)(4,1)}), s8[4194304]{0:T(1024)(128)(4,1)S(1)}, s32[]{:S(2)}) async-start(s8[8388608]{0:T(1024)(128)(4,1)} %bitcast.363), calls=%async_computation.28 | async-start | bytes 8388608
  541.5 14.6 %slice-start.6 = ((s8[8388608]{0:T(1024)(128)(4,1)}), s8[4194304]{0:T(1024)(128)(4,1)S(1)}, s32[]{:S(2)}) async-start(s8[8388608]{0:T(1024)(128)(4,1)} %bitcast.365), calls=%async_computation.30 | async-start | bytes 8388608
  541.5 15.7 %slice-start.5 = ((s8[8388608]{0:T(1024)(128)(4,1)}), s8[4194304]{0:T(1024)(128)(4,1)S(1)}, s32[]{:S(2)}) async-start(s8[8388608]{0:T(1024)(128)(4,1)} %bitcast.363), calls=%async_computation.29 | async-start | bytes 8388608
  541.5 17.0 %slice-start.7 = ((s8[8388608]{0:T(1024)(128)(4,1)}), s8[4194304]{0:T(1024)(128)(4,1)S(1)}, s32[]{:S(2)}) async-start(s8[8388608]{0:T(1024)(128)(4,1)} %bitcast.365), calls=%async_computation.31 | async-start | bytes 8388608
  583.0 14.2 %slice-start = ((s8[8388608]{0:T(1024)(128)(4,1)}), s8[4194304]{0:T(1024)(128)(4,1)S(1)}, s32[]{:S(2)}) async-start(s8[8388608]{0:T(1024)(128)(4,1)} %bitcast.359), calls=%async_computation.24 | async-start | bytes 8388608
  583.0 14.2 %slice-start.2 = ((s8[8388608]{0:T(1024)(128)(4,1)}), s8[4194304]{0:T(1024)(128)(4,1)S(1)}, s32[]{:S(2)}) async-start(s8[8388608]{0:T(1024)(128)(4,1)} %bitcast.361), calls=%async_computation.26 | async-start | bytes 8388608
  583.0 15.2 %slice-start.1 = ((s8[8388608]{0:T(1024)(128)(4,1)}), s8[4194304]{0:T(1024)(128)(4,1)S(1)}, s32[]{:S(2)}) async-start(s8[8388608]{0:T(1024)(128)(4,1)} %bitcast.359), calls=%async_computation.25 | async-start | bytes 8388608
  583.0 16.4 %slice-start.3 = ((s8[8388608]{0:T(1024)(128)(4,1)}), s8[4194304]{0:T(1024)(128)(4,1)S(1)}, s32[]{:S(2)}) async-start(s8[8388608]{0:T(1024)(128)(4,1)} %bitcast.361), calls=%async_computation.27 | async-start | bytes 8388608
  599.4 10.1 %copy-start.18 = (bf16[1024,4,64]{0,2,1:T(8,128)(2,1)S(1)}, bf16[1024,4,64]{0,2,1:T(8,128)(2,1)}, u32[]{:S(2)}) copy-start(bf16[1024,4,64]{0,2,1:T(8,128)(2,1)} %copy-done.17) | copy-start | bytes 1572868
  677.1 65.8 %reduce-scatter.20.cloned.1.call-start = ((), (), s32[]{:S(2)}) async-start(), calls=%async_computation.18 | async-start | bytes 2621440 | tf_op jit(solution)/shard_map/reduce_scatter | solution.py:129
  711.0 270.9 %reduce-scatter.26.cloned.1.call-start = ((), (), s32[]{:S(2)}) async-start(), calls=%async_computation.23 | async-start | bytes 8257536 | tf_op jit(solution)/shard_map/reduce_scatter | solution.py:77
  733.0 9.9 copy-start.103
  733.0 9.9 copy-start.105
  733.0 9.9 copy-start.109
  741.7 13.9 %copy-start.11 = (bf16[1024,256]{1,0:T(8,128)(2,1)S(1)}, bf16[1024,256]{1,0:T(8,128)(2,1)}, u32[]{:S(2)}) copy-start(bf16[1024,256]{1,0:T(8,128)(2,1)} %reduce-scatter.10.cloned.1.call-done) | copy-start | bytes 1572868
  849.8 40.5 %copy-start.107 = (f32[13,256]{1,0:T(8,128)S(1)}, f32[13,256]{1,0:T(8,128)}, u32[]{:S(2)}) copy-start(f32[13,256]{1,0:T(8,128)} %param.29) | copy-start | bytes 39940
  849.8 40.5 %copy-start.118 = (f32[13,256]{1,0:T(8,128)S(1)}, f32[13,256]{1,0:T(8,128)}, u32[]{:S(2)}) copy-start(f32[13,256]{1,0:T(8,128)} %param.31) | copy-start | bytes 39940
  849.8 40.5 %copy-start.119 = (f32[13,256]{1,0:T(8,128)S(1)}, f32[13,256]{1,0:T(8,128)}, u32[]{:S(2)}) copy-start(f32[13,256]{1,0:T(8,128)} %param.30) | copy-start | bytes 39940
  850.1 40.8 %copy-start.52 = (bf16[1024,256]{1,0:T(8,128)(2,1)S(1)}, bf16[1024,256]{1,0:T(8,128)(2,1)}, u32[]{:S(2)}) copy-start(bf16[1024,256]{1,0:T(8,128)(2,1)} %reduce-scatter.20.cloned.1.call-done) | copy-start | bytes 1572868
  892.8 91.4 %copy-start.71 = (f32[128,14,256]{2,0,1:T(8,128)S(1)}, f32[128,14,256]{2,0,1:T(8,128)}, u32[]{:S(2)}) copy-start(f32[128,14,256]{2,0,1:T(8,128)} %param.25) | copy-start | bytes 5505028
  (125 other events, 433.5 us)
Sparse Core Ops, SparseCore 0:
  10.8 63.1 all-gather.6
  76.2 71.9 all-gather.8
  223.5 29.7 reduce-scatter.13
  255.8 31.4 reduce-scatter.9
  288.7 25.3 all-gather.14
  315.5 24.1 all-gather.10
  354.1 34.7 reduce-scatter.21
  407.3 31.3 reduce-scatter.17
  441.2 31.3 reduce-scatter.15
  475.1 31.4 reduce-scatter.11
  510.9 22.8 all-gather.16
  535.2 22.8 all-gather.12
  677.3 31.6 reduce-scatter.23
  711.5 31.3 reduce-scatter.19
  847.4 134.4 reduce-scatter.25
